TPU v7x, 32 devices: a whole 2x2x4 slice. The times are simulated.
32 devices in a mesh: groups: 2 (over y), wide: 4 (over z), narrow: 4 (over x, core).
Axes of the slice: x: 2, y: 2, z: 4, core: 2. Of those that a mesh axis runs over, the one named last changes fastest.
Arguments:
- inputs: bfloat16 [40, 2, 8192], P('groups', None, 'narrow'), parts along dimension 0, may hold values from -6 to 6
- xz_weight: bfloat16 [8192, 2, 16384], P('narrow', None, 'wide'), may hold values from -0.0625 to 0.0625
- bc_weight: bfloat16 [8192, 4096], P('narrow', 'wide'), may hold values from -0.0625 to 0.0625
- dt_weight: bfloat16 [8192, 256], P('narrow', 'wide'), may hold values from -0.0625 to 0.0625
- conv_x_weight: bfloat16 [4, 256, 64], P(None, 'wide', 'narrow'), may hold values from -3 to 3
- conv_x_bias: bfloat16 [256, 64], P('wide', 'narrow'), may hold values from -3 to 3
- conv_bc_weight: bfloat16 [4, 4096], P(None, 'wide'), may hold values from -3 to 3
- conv_bc_bias: bfloat16 [4096], P('wide'), may hold values from -3 to 3
- conv_x_state: bfloat16 [40, 3, 256, 64], P('groups', None, 'wide', 'narrow'), parts along dimension 0, may hold values from -6 to 6
- conv_bc_state: bfloat16 [40, 3, 4096], P('groups', None, 'wide'), parts along dimension 0, may hold values from -6 to 6
- dt_bias: float32 [256], P('wide'), may hold values from -4 to 0
- a_log: float32 [256], P('wide'), may hold values from 0 to 2.5
- d_skip: float32 [256], P('wide'), may hold values from 0.5 to 2
- norm_weight: bfloat16 [256, 64], P('wide', 'narrow'), may hold values from 0.099609375 to 1.8984375
- out_weight: bfloat16 [256, 64, 8192], P(None, 'narrow', 'wide'), may hold values from -0.046875 to 0.046875
- ssm_state: float32 [40, 256, 64, 256], P('groups', 'wide', 'narrow'), parts along dimension 0, may hold values from -4 to 4
Outputs:
- layer_out: bfloat16 [40, 2, 8192], P('groups', None, ('wide', 'narrow')), parts along dimension 0
- new_ssm_state: float32 [40, 256, 64, 256], P('groups', 'wide', 'narrow'), parts along dimension 0
- new_conv_x: bfloat16 [40, 3, 256, 64], P('groups', None, 'wide', 'narrow'), parts along dimension 0
- new_conv_bc: bfloat16 [40, 3, 4096], P('groups', None, 'wide'), parts along dimension 0
There are 2 independent parts, one for each index of `groups`. A program takes and returns all parts, laid end to end along the dimension named above; an argument that names none is the same for every part. Nothing has to cross between parts.
All inputs are finite; a program needn't handle non-finite values.
Results may differ from a plain program's by a relative error of at most 0.015.
Values may be sent and summed in bfloat16 or wider, within the bound.
A program may use at most 192 MiB of HBM per device.

v0:
```python
import jax
import jax.numpy as jnp
from jax import lax
from jax.sharding import PartitionSpec as P

HEADS = 256
HEAD_DIM = 64
STATE = 256
NGROUPS = 8
EPSILON = 1e-05


def shortened(value):

    def short(part):
        return part.astype(jnp.bfloat16) if part.dtype == jnp.float32 else part

    return jax.tree.map(short, value)


def swapped(value, axis, bit):
    mask = 2**bit
    pairs = [(source, source ^ mask) for source in range(lax.axis_size(axis))]
    return lax.ppermute(value, axis, pairs)


def conv_tokens(history, fresh_vals, tap_weights, offset):
    window = jnp.concatenate([history, fresh_vals], axis=1)
    outputs = []
    for token_idx in range(2):
        summed = offset.astype(jnp.float32)
        for tap_idx in range(tap_weights.shape[0]):
            summed = summed + tap_weights[tap_idx].astype(jnp.float32) * window[
                :, token_idx + tap_idx
            ].astype(jnp.float32)
        outputs.append(jax.nn.silu(summed))
    return (jnp.stack(outputs, axis=1), window[:, 2:])


def advance(ssm_now, x_tok, b_tok, c_tok, dt_tok, dt_bias, a_log, d_skip):
    step_size = jax.nn.softplus(dt_tok.astype(jnp.float32) + dt_bias)
    decay_now = jnp.exp(-step_size * jnp.exp(a_log))
    inject = (step_size[:, :, None] * x_tok)[..., None] * b_tok[:, :, None, :]
    ssm_now = decay_now[:, :, None, None] * ssm_now + inject
    readout = jnp.sum(ssm_now * c_tok[:, :, None, :], axis=-1) + d_skip[None, :, None] * x_tok
    return (ssm_now, readout)


def shards(
    inputs,
    xz_weight,
    bc_weight,
    dt_weight,
    conv_x_weight,
    conv_x_bias,
    conv_bc_weight,
    conv_bc_bias,
    conv_x_state,
    conv_bc_state,
    dt_bias,
    a_log,
    d_skip,
    norm_weight,
    out_weight,
    ssm_state,
):
    seq_count = inputs.shape[0]
    row_count = seq_count * 2
    tok_rows = inputs.reshape(row_count, inputs.shape[2])
    head_local = dt_weight.shape[1]
    wide_count = lax.axis_size("wide")
    narrow_count = lax.axis_size("narrow")
    wide_index = lax.axis_index("wide")
    chan_local = HEAD_DIM // narrow_count
    xz_local = xz_weight.reshape(xz_weight.shape[0], 2, head_local, HEAD_DIM)
    bc_part = jnp.dot(tok_rows, bc_weight, preferred_element_type=jnp.float32)
    dt_part = jnp.dot(tok_rows, dt_weight, preferred_element_type=jnp.float32)
    xz_mine = lax.psum_scatter(
        jnp.einsum("rd,dzhc->czrh", tok_rows, xz_local, preferred_element_type=jnp.float32),
        "narrow",
        scatter_dimension=0,
        tiled=True,
    )
    bc_summed, dt_summed = lax.psum((bc_part, dt_part), "narrow")
    xz_mine = xz_mine.astype(jnp.bfloat16)
    xz_mine = jnp.transpose(xz_mine, (1, 2, 3, 0)).reshape(2, seq_count, 2, head_local, chan_local)
    gate_vals = xz_mine[0]
    x_proj = xz_mine[1]
    bc_proj = bc_summed.astype(jnp.bfloat16).reshape(seq_count, 2, bc_summed.shape[1])
    dt_proj = dt_summed.astype(jnp.bfloat16).reshape(seq_count, 2, head_local)
    x_conv, new_conv_x = conv_tokens(conv_x_state, x_proj, conv_x_weight, conv_x_bias)
    bc_conv, new_conv_bc = conv_tokens(conv_bc_state, bc_proj, conv_bc_weight, conv_bc_bias)
    group_local = max(NGROUPS // wide_count, 1)
    group_span = max(wide_count // NGROUPS, 1)
    bc_mine = bc_conv.reshape(row_count, bc_conv.shape[2])
    for bit_idx in range(group_span.bit_length() - 1):
        partner = swapped(shortened(bc_mine), "wide", bit_idx).astype(bc_mine.dtype)
        is_lower = wide_index // (1 << bit_idx) % 2 == 0
        bc_mine = jnp.where(
            is_lower,
            jnp.concatenate([bc_mine, partner], axis=1),
            jnp.concatenate([partner, bc_mine], axis=1),
        )
    bc_heads = bc_mine.reshape(seq_count, 2, group_local, 2, STATE)
    per_group = head_local // group_local
    b_heads = jnp.repeat(bc_heads[:, :, :, 0], per_group, axis=2)
    c_heads = jnp.repeat(bc_heads[:, :, :, 1], per_group, axis=2)
    ssm_now = ssm_state
    readouts = []
    for token_idx in range(2):
        ssm_now, readout = advance(
            ssm_now,
            x_conv[:, token_idx],
            b_heads[:, token_idx],
            c_heads[:, token_idx],
            dt_proj[:, token_idx],
            dt_bias,
            a_log,
            d_skip,
        )
        readouts.append(readout)
    y_all = jnp.stack(readouts, axis=1)
    gated_out = y_all * jax.nn.silu(gate_vals.astype(jnp.float32))
    grouped = gated_out.reshape(seq_count, 2, group_local, per_group * chan_local)
    squares_part = jnp.sum(grouped * grouped, axis=-1)
    group_sum = lax.psum(squares_part, "narrow")
    for bit_idx in range(group_span.bit_length() - 1):
        group_sum = group_sum + swapped(group_sum, "wide", bit_idx)
    inverse = lax.rsqrt(group_sum / (HEADS // NGROUPS * HEAD_DIM) + EPSILON)
    normed = (grouped * inverse[..., None]).reshape(
        seq_count, 2, head_local, chan_local
    ) * norm_weight.astype(jnp.float32)
    normed = normed.astype(jnp.bfloat16).reshape(row_count, head_local, chan_local)
    out_part = jnp.einsum(
        "rhc,hcd->rd",
        lax.all_gather(normed, "wide", axis=1, tiled=True),
        out_weight,
        preferred_element_type=jnp.float32,
    )
    out_mine = lax.psum_scatter(
        out_part.astype(jnp.bfloat16), "narrow", scatter_dimension=1, tiled=True
    )
    layer_out = out_mine.reshape(seq_count, 2, out_mine.shape[1])
    return (layer_out, ssm_now, new_conv_x, new_conv_bc)


def solution(mesh):
    return jax.shard_map(
        shards,
        mesh=mesh,
        in_specs=(
            P("groups", None, "narrow"),
            P("narrow", None, "wide"),
            P("narrow", "wide"),
            P("narrow", "wide"),
            P(None, "wide", "narrow"),
            P("wide", "narrow"),
            P(None, "wide"),
            P("wide"),
            P("groups", None, "wide", "narrow"),
            P("groups", None, "wide"),
            P("wide"),
            P("wide"),
            P("wide"),
            P("wide", "narrow"),
            P(None, "narrow", "wide"),
            P("groups", "wide", "narrow", None),
        ),
        out_specs=(
            P("groups", None, ("wide", "narrow")),
            P("groups", "wide", "narrow", None),
            P("groups", None, "wide", "narrow"),
            P("groups", None, "wide"),
        ),
        check_vma=False,
    )
```

profile of v0, /device:TPU:0, one launch (start us, length us, event | category | flops | bytes accessed | tf_op | source)
XLA Modules:
  0.0 250.9 jit_solution(5239584444995894743)
XLA Ops:
  7.2 0.0 reduce-scatter.3.cloned.1.call-start
  7.2 80.9 %copy.186 = bf16[2048,2,4096]{0,2,1:T(8,128)(2,1)} copy(bf16[2048,2,4096]{2,1,0:T(2,128)(2,1)} %param.17) | data formatting | bytes 67108864 | tf_op args[1]
  88.2 0.1 reshape.347
  88.3 21.7 %convolution_bitcast_fusion.1 = f32[64,2,40,64]{0,2,3,1:T(8,128)S(1)} fusion(bf16[2048,2,64,64]{0,3,2,1:T(8,128)(2,1)} %bitcast.177, bf16[40,2048,1,1]{1,0,2,3:T(8,128)(2,1)S(1)} %reshape.347), kind=kOutput, calls=%fused_computation.6 | convolution fusion | flops 1342177280 | bytes 35028992 | tf_op jit(solution)/shard_map/rd,dzhc->czrh/dot_general | solution.py:79
  110.0 2.1 copy.187
  112.1 0.0 reduce-scatter.5.cloned.1.call-start
  112.1 0.1 reshape.324
  112.2 3.0 %fusion.60 = f32[40,1024]{1,0:T(8,128)S(1)} fusion(bf16[40,2048]{1,0:T(8,128)(2,1)S(1)} %reshape.324, bf16[2048,1024]{1,0:T(8,128)(2,1)} %param.18), kind=kOutput, calls=%fused_computation.124 | convolution fusion | flops 167772160 | bytes 4521984 | tf_op jit(solution)/shard_map/dot_general | solution.py:76
  115.2 0.2 fusion.59
  115.5 15.5 %all-reduce.2 = (bf16[40,1024]{1,0:T(8,128)(2,1)S(1)}, bf16[40,64]{1,0:T(8,128)(2,1)S(1)}) all-reduce(f32[40,1024]{1,0:T(8,128)S(1)} %fusion.60, f32[40,64]{1,0:T(8,128)S(1)} %fusion.59), channel_id=1, replica_groups=mesh['groups'=2,'wide'=4,'narrow'=4] {'narrow'}, use_global_device_ids=true, to_apply=%region_2.0 | all-reduce | flops 43520 | bytes 261120 | tf_op jit(solution)/shard_map/psum | solution.py:84
  131.1 0.6 copy-done.9
  131.7 1.0 divide_multiply_fusion
  132.7 0.1 stack.24
  132.8 0.1 stack.25
  132.9 0.2 copy.216
  133.1 0.2 copy.215
  133.3 0.9 copy.214
  134.2 0.7 copy.185
  134.9 0.7 copy.183
  135.6 0.7 copy.181
  136.3 0.7 copy.179
  137.0 1.4 copy.178
  138.4 0.7 exp.82
  139.0 1.3 convert_element_type.253
  140.3 1.3 multiply_exponential_fusion
  141.6 0.1 fusion.57
  141.8 0.1 copy_bitcast_fusion
  141.9 0.2 broadcast_in_dim.5
  142.1 0.3 slice_bitcast_fusion.2
  142.4 0.2 broadcast_in_dim.4
  142.6 1.8 slice_bitcast_fusion.3
  144.4 5.1 %reduce-scatter.3.cloned.1.call-done = f32[16,2,40,64]{3,2,1,0:T(8,128)} async-done(((f32[64,2,40,64]{3,2,1,0:T(8,128)}), f32[16,2,40,64]{3,2,1,0:T(8,128)}) %reduce-scatter.3.cloned.1.call-update) | async-done | bytes 327696 | tf_op jit(solution)/shard_map/reduce_scatter | solution.py:78
  149.5 1.3 copy.234
  150.8 0.7 copy-done.4
  151.5 0.7 copy-done.5
  152.2 0.7 fusion.56
  152.8 1.8 copy.217
  154.6 1.8 copy.218
  156.4 2.0 multiply_multiply_fusion.1
  158.5 21.2 %multiply_reduce_fusion = (f32[20,64,16]{2,1,0:T(8,128)S(1)}, f32[20,64,16,256]{3,2,1,0:T(8,128)}, f32[20,64,16]{2,1,0:T(8,128)S(1)}) fusion(f32[20,64,256]{2,1,0:T(8,128)S(1)} %get-tuple-element.10, f32[20,64,256]{2,1,0:T(8,128)} %get-tuple-element.12, f32[20,64,16]{2,1,0:T(8,128)S(1)} %get-tuple-element.16, f32[20,64,256]{2,1,0:T(8,128)} %get-tuple-element.11, ...), kind=kLoop, calls=%fused_computation | loop fusion | flops 52387840 | bytes 47523840 | tf_op jit(solution)/shard_map/reduce_sum | solution.py:45
  179.7 0.8 bitcast_add_fusion.1
  180.5 0.2 copy.199
  180.7 0.4 stack.30
  181.1 0.2 copy.198
  181.3 0.4 stack.29
  181.7 0.1 pad_maximum_fusion.2
  181.8 0.5 stack.32
  182.3 0.4 copy.201
  182.7 1.1 fusion.40
  183.8 0.1 reduce_sum.43
  183.9 0.1 reduce_sum.44
  184.0 0.1 copy.204
  184.1 5.7 %psum.23 = f32[20,2,2]{0,2,1:T(2,128)S(1)} all-reduce(f32[20,2,2]{0,2,1:T(2,128)S(1)} %copy.204), channel_id=1, replica_groups=mesh['groups'=2,'wide'=4,'narrow'=4] {'narrow'}, use_global_device_ids=true, to_apply=%region_7.8 | all-reduce | flops 80 | bytes 640 | tf_op jit(solution)/shard_map/psum | solution.py:126
  189.9 0.1 copy.205
  190.0 0.1 mul.491
  190.1 0.1 mul.492
  190.2 1.1 fusion.39
  191.3 0.3 copy.206
  191.6 22.6 %all_gather.3 = bf16[40,256,16]{0,2,1:T(8,128)(2,1)S(1)} all-gather(bf16[40,64,16]{0,2,1:T(8,128)(2,1)S(1)} %copy.206), channel_id=1, replica_groups=mesh['groups'=2,'wide'=4,'narrow'=4] {'wide'}, dimensions={1}, use_global_device_ids=true | all-gather | bytes 409600 | tf_op jit(solution)/shard_map/all_gather | solution.py:136
  214.3 9.5 %fusion = bf16[40,2048]{1,0:T(8,128)(2,1)} fusion(bf16[40,256,16]{0,2,1:T(8,128)(2,1)S(1)} %all_gather.3, bf16[256,16,2048]{2,1,0:T(8,128)(2,1)} %param.30), kind=kOutput, calls=%fused_computation.5 | convolution fusion | flops 671170560 | bytes 17268736 | tf_op jit(solution)/shard_map/rhc,hcd->rd/dot_general | solution.py:134
  223.8 0.7 pad_maximum_fusion.3
  224.5 0.7 pad_maximum_fusion.1
  225.3 17.4 %reduce-scatter.5.cloned.1.call-done = bf16[40,512]{1,0:T(8,128)(2,1)} async-done(((bf16[40,2048]{1,0:T(8,128)(2,1)}), bf16[40,512]{1,0:T(8,128)(2,1)}) %reduce-scatter.5.cloned.1.call-update) | async-done | bytes 40976 | tf_op jit(solution)/shard_map/reduce_scatter | solution.py:140
  242.7 1.4 reshape.330
  (56 shorter events, 0.3 us)
Async XLA Ops:
  7.2 108.1 %copy-start = (bf16[2048,64]{0,1:T(8,128)(2,1)S(1)}, bf16[2048,64]{0,1:T(8,128)(2,1)}, u32[]{:S(2)}) copy-start(bf16[2048,64]{0,1:T(8,128)(2,1)} %param.19) | copy-start | bytes 786436
  7.2 81.0 %copy-start.11 = (bf16[20,2,2048]{2,1,0:T(2,128)(2,1)S(1)}, bf16[20,2,2048]{2,1,0:T(2,128)(2,1)}, u32[]{:S(2)}) copy-start(bf16[20,2,2048]{2,1,0:T(2,128)(2,1)} %param.16) | copy-start | bytes 491524
  7.2 142.3 %reduce-scatter.3.cloned.1.call-start = ((), (), s32[]{:S(2)}) async-start(), calls=%async_computation.2 | async-start | bytes 3276800 | tf_op jit(solution)/shard_map/reduce_scatter | solution.py:78
  88.2 42.8 %copy-start.20 = (bf16[1024]{0:T(1024)(128)(2,1)S(1)}, bf16[1024]{0:T(1024)(128)(2,1)}, u32[]{:S(2)}) copy-start(bf16[1024]{0:T(1024)(128)(2,1)} %param.23) | copy-start | bytes 6148
  88.2 42.8 %copy-start.18 = (bf16[4,1024]{1,0:T(4,128)(2,1)S(1)}, bf16[4,1024]{1,0:T(4,128)(2,1)}, u32[]{:S(2)}) copy-start(bf16[4,1024]{1,0:T(4,128)(2,1)} %param.22) | copy-start | bytes 24580
  88.3 44.6 %copy-start.7 = (bf16[20,3,64,16]{2,3,1,0:T(8,128)(2,1)S(1)}, bf16[20,3,64,16]{2,3,1,0:T(8,128)(2,1)}, u32[]{:S(2)}) copy-start(bf16[20,3,64,16]{2,3,1,0:T(8,128)(2,1)} %param.24) | copy-start | bytes 368644
  88.3 45.9 %copy-start.19 = (bf16[4,64,16]{1,2,0:T(8,128)(2,1)S(1)}, bf16[4,64,16]{1,2,0:T(8,128)(2,1)}, u32[]{:S(2)}) copy-start(bf16[4,64,16]{1,2,0:T(8,128)(2,1)} %param.20) | copy-start | bytes 24580
  112.1 130.6 %reduce-scatter.5.cloned.1.call-start = ((), (), s32[]{:S(2)}) async-start(), calls=%async_computation.3 | async-start | bytes 204800 | tf_op jit(solution)/shard_map/reduce_scatter | solution.py:140
  131.0 0.6 copy-start.9
  150.8 0.7 copy-start.4
  151.5 0.7 copy-start.5
  158.4 21.3 %copy-start.1 = (bf16[20,1,64,16]{3,2,0,1:T(8,128)(2,1)S(1)}, bf16[20,1,64,16]{3,2,0,1:T(8,128)(2,1)}, u32[]{:S(2)}) copy-start(bf16[20,1,64,16]{3,2,0,1:T(8,128)(2,1)} %copy.214) | copy-start | bytes 122884
  158.4 21.3 %copy-start.2 = (bf16[20,1,64,16]{3,2,0,1:T(8,128)(2,1)S(1)}, bf16[20,1,64,16]{3,2,0,1:T(8,128)(2,1)}, u32[]{:S(2)}) copy-start(bf16[20,1,64,16]{3,2,0,1:T(8,128)(2,1)} %copy.217) | copy-start | bytes 122884
  158.4 21.3 %copy-start.3 = (bf16[20,1,64,16]{3,2,0,1:T(8,128)(2,1)S(1)}, bf16[20,1,64,16]{3,2,0,1:T(8,128)(2,1)}, u32[]{:S(2)}) copy-start(bf16[20,1,64,16]{3,2,0,1:T(8,128)(2,1)} %copy.218) | copy-start | bytes 122884
  158.4 21.3 %copy-start.13 = (f32[64,16]{1,0:T(8,128)S(1)}, f32[64,16]{1,0:T(8,128)}, u32[]{:S(2)}) copy-start(f32[64,16]{1,0:T(8,128)} %copy.185) | copy-start | bytes 12292
  158.4 21.3 %copy-start.14 = (f32[64,16]{1,0:T(8,128)S(1)}, f32[64,16]{1,0:T(8,128)}, u32[]{:S(2)}) copy-start(f32[64,16]{1,0:T(8,128)} %copy.183) | copy-start | bytes 12292
  158.4 21.3 %copy-start.15 = (f32[64,16]{1,0:T(8,128)S(1)}, f32[64,16]{1,0:T(8,128)}, u32[]{:S(2)}) copy-start(f32[64,16]{1,0:T(8,128)} %copy.181) | copy-start | bytes 12292
  158.5 21.3 %copy-start.16 = (f32[64,16]{1,0:T(8,128)S(1)}, f32[64,16]{1,0:T(8,128)}, u32[]{:S(2)}) copy-start(f32[64,16]{1,0:T(8,128)} %copy.179) | copy-start | bytes 12292
  158.5 21.3 %copy-start.17 = (f32[64,16]{1,0:T(8,128)S(1)}, f32[64,16]{1,0:T(8,128)}, u32[]{:S(2)}) copy-start(f32[64,16]{1,0:T(8,128)} %copy.178) | copy-start | bytes 12292
  158.5 21.3 %copy-start.21 = (f32[64]{0:T(128)S(1)}, f32[64]{0:T(128)}, u32[]{:S(2)}) copy-start(f32[64]{0:T(128)} %param.28) | copy-start | bytes 772
  181.7 42.1 %copy-start.10 = (bf16[20,2,1024]{2,0,1:T(8,128)(2,1)S(1)}, bf16[20,2,1024]{2,0,1:T(8,128)(2,1)}, u32[]{:S(2)}) copy-start(bf16[20,2,1024]{2,0,1:T(8,128)(2,1)} %copy-done.9) | copy-start | bytes 245764
  181.7 42.1 %copy-start.12 = (bf16[20,3,1024]{2,0,1:T(8,128)(2,1)S(1)}, bf16[20,3,1024]{2,0,1:T(8,128)(2,1)}, u32[]{:S(2)}) copy-start(bf16[20,3,1024]{2,0,1:T(8,128)(2,1)} %param.25) | copy-start | bytes 368644
  181.8 42.7 %copy-start.6 = (bf16[1,40,64,16]{2,3,1,0:T(8,128)(2,1)S(1)}, bf16[1,40,64,16]{2,3,1,0:T(8,128)(2,1)}, u32[]{:S(2)}) copy-start(bf16[1,40,64,16]{2,3,1,0:T(8,128)(2,1)} %copy-done.5) | copy-start | bytes 245764
  181.8 42.7 %copy-start.8 = (bf16[20,3,64,16]{2,3,1,0:T(8,128)(2,1)S(1)}, bf16[20,3,64,16]{2,3,1,0:T(8,128)(2,1)}, u32[]{:S(2)}) copy-start(bf16[20,3,64,16]{2,3,1,0:T(8,128)(2,1)} %param.24) | copy-start | bytes 368644
Sparse Core Ops, SparseCore 0:
  112.2 37.1 reduce-scatter.2
  223.9 18.6 reduce-scatter.4
where the time goes:
time: 254 us; the launch traced here: 251 us
  local copies, waits for them, and re-layouts  104 us (41%)
  blocking collectives  43.9 us (17%)
  matrix products  34.4 us (14%)
  other arithmetic  31.4 us (12%)
  waiting for transfers between devices  22.5 us (9%)
  between operations  14.6 us (6%)
    unnamed x52, local copies, waits for them, and re-layouts  87.9 us
    all_gather x1, blocking collectives, shards(): lax.all_gather(normed, 'wide', axis=1, tiled=True)  22.6 us
    dot_general x1, matrix products, shards(): jnp.einsum('rd,dzhc->czrh', tok_rows, xz_local, preferred_element_type=jn...  21.7 us
    reduce_sum x1, other arithmetic, advance(): jnp.sum(ssm_now * c_tok[:, :, None, :], axis=-1)  21.2 us
    reduce_scatter x1, waiting for transfers between devices, shards(): lax.psum_scatter(out_part.astype(jnp.bfloat16), 'narrow', scatter_dimensi...  17.4 us
    psum x1, blocking collectives, shards(): bc_summed, dt_summed = lax.psum((bc_part, dt_part), 'narrow')  15.5 us
    dot_general x1, matrix products, shards(): jnp.einsum('rhc,hcd->rd', lax.all_gather(normed, 'wide', axis=1, tiled=Tr...  9.51 us
    psum x1, blocking collectives, shards(): group_sum = lax.psum(squares_part, 'narrow')  5.73 us
  transfers between devices with their start and end apart: 2, of which 2 were waited for; matrix products, arithmetic and copies ran while one was open for 7% of the time, Pallas kernels for 0%

commit v1 on v0

--- a/solution.py
+++ b/solution.py
@@ -8,6 +8,22 @@
 STATE = 256
 NGROUPS = 8
 EPSILON = 1e-05
+
+
+def ring_gather(x, axis, dim):
+    ways, here, hop = (lax.axis_size(axis), lax.axis_index(axis), x.shape[dim])
+    lengths = [n * ways if d == dim else n for d, n in enumerate(x.shape)]
+    full = lax.dynamic_update_slice_in_dim(jnp.zeros(lengths, x.dtype), x, here * hop, axis=dim)
+    going_up = going_down = x
+    for far in range(1, ways // 2 + 1):
+        going_up = lax.ppermute(going_up, axis, [(d, (d + 1) % ways) for d in range(ways)])
+        full = lax.dynamic_update_slice_in_dim(full, going_up, (here - far) % ways * hop, axis=dim)
+        if 2 * far < ways:
+            going_down = lax.ppermute(going_down, axis, [(d, (d - 1) % ways) for d in range(ways)])
+            full = lax.dynamic_update_slice_in_dim(
+                full, going_down, (here + far) % ways * hop, axis=dim
+            )
+    return full
 
 
 def shortened(value):
@@ -133,7 +149,7 @@
     normed = normed.astype(jnp.bfloat16).reshape(row_count, head_local, chan_local)
     out_part = jnp.einsum(
         "rhc,hcd->rd",
-        lax.all_gather(normed, "wide", axis=1, tiled=True),
+        ring_gather(normed, "wide", 1),
         out_weight,
         preferred_element_type=jnp.float32,
     )

time: 254 us -> 272 us (1.071)
  blocking collectives: 43.9 us -> 21.2 us
  matrix products: 34.4 us -> 53.5 us
  local copies, waits for them, and re-layouts: 104 us -> 114 us
  waiting for transfers between devices: 22.5 us -> 32.3 us
  starting transfers between devices: 0.08 us -> 3.96 us
    all_gather x1 -> x0, blocking collectives: 22.6 us -> none  [shards(): lax.all_gather(normed, 'wide', axis=1, tiled=True)]
    dot_general x1, matrix products: 9.51 us -> 28.5 us  [shards(): jnp.einsum('rhc,hcd->rd', ring_gather(normed, 'wide', 1), out_weight, pre...]
    dynamic_update_slice x0 -> x4, local copies, waits for them, and re-layouts: none -> 11.4 us  [the longest x2 5.47 us: ring_gather(): lax.dynamic_update_slice_in_dim(full, going_up, (here - far) % ways * hop...]
    ppermute x0 -> x3, waiting for transfers between devices: none -> 5.1 us  [the longest x2 5.1 us: ring_gather(): lax.ppermute(going_up, axis, [(d, (d + 1) % ways) for d in range(ways)])]
    ppermute x0 -> x3, starting transfers between devices: none -> 3.88 us  [the longest x1 2.17 us: ring_gather(): lax.ppermute(going_down, axis, [(d, (d - 1) % ways) for d in range(ways)])]
    reduce_scatter x1, waiting for transfers between devices: 5.09 us -> 7.81 us  [shards(): lax.psum_scatter(jnp.einsum('rd,dzhc->czrh', tok_rows, xz_local, preferre...]
    unnamed x52 -> x60, local copies, waits for them, and re-layouts: 87.9 us -> 88 us
  transfers between devices with their start and end apart: 2 -> 5, of which waited for: 2 -> 3; matrix products, arithmetic and copies ran while one was open for 7% -> 9% of each run, Pallas kernels for 0% -> 0%
where the time goes in v1:
time: 272 us; the launch traced here: 270 us
  local copies, waits for them, and re-layouts  114 us (42%)
  matrix products  53.5 us (20%)
  waiting for transfers between devices  32.3 us (12%)
  other arithmetic  30.1 us (11%)
  blocking collectives  21.2 us (8%)
  between operations  14.7 us (5%)
  starting transfers between devices  3.96 us (1%)
    unnamed x60, local copies, waits for them, and re-layouts  88 us
    dot_general x1, matrix products, shards(): jnp.einsum('rhc,hcd->rd', ring_gather(normed, 'wide', 1), out_weight, pre...  28.5 us
    dot_general x1, matrix products, shards(): jnp.einsum('rd,dzhc->czrh', tok_rows, xz_local, preferred_element_type=jn...  21.7 us
    reduce_sum x1, other arithmetic, advance(): jnp.sum(ssm_now * c_tok[:, :, None, :], axis=-1)  21.2 us
    reduce_scatter x1, waiting for transfers between devices, shards(): lax.psum_scatter(out_part.astype(jnp.bfloat16), 'narrow', scatter_dimensi...  19.4 us
    psum x1, blocking collectives, shards(): bc_summed, dt_summed = lax.psum((bc_part, dt_part), 'narrow')  15.5 us
    reduce_scatter x1, waiting for transfers between devices, shards(): lax.psum_scatter(jnp.einsum('rd,dzhc->czrh', tok_rows, xz_local, preferre...  7.81 us
    psum x1, blocking collectives, shards(): group_sum = lax.psum(squares_part, 'narrow')  5.73 us
  transfers between devices with their start and end apart: 5, of which 3 were waited for; matrix products, arithmetic and copies ran while one was open for 9% of the time, Pallas kernels for 0%

profile of v1, /device:TPU:0, one launch (start us, length us, event | category | flops | bytes accessed | tf_op | source)
XLA Modules:
  0.0 269.7 jit_solution(5974984070286842549)
XLA Ops:
  7.2 81.0 %copy.210 = bf16[2048,2,4096]{0,2,1:T(8,128)(2,1)} copy(bf16[2048,2,4096]{2,1,0:T(2,128)(2,1)} %param.17) | data formatting | bytes 67108864 | tf_op args[1]
  88.4 21.7 %convolution_bitcast_fusion = f32[64,2,40,64]{0,2,3,1:T(8,128)S(1)} fusion(bf16[2048,2,64,64]{0,3,2,1:T(8,128)(2,1)} %bitcast.176, bf16[40,2048,1,1]{1,0,2,3:T(8,128)(2,1)S(1)} %reshape.347), kind=kOutput, calls=%fused_computation.8 | convolution fusion | flops 1342177280 | bytes 35028992 | tf_op jit(solution)/shard_map/rd,dzhc->czrh/dot_general | solution.py:95
  110.1 2.1 copy.211
  112.3 3.0 %fusion.67 = f32[40,1024]{1,0:T(8,128)S(1)} fusion(bf16[40,2048]{1,0:T(8,128)(2,1)S(1)} %reshape.324, bf16[2048,1024]{1,0:T(8,128)(2,1)} %param.18), kind=kOutput, calls=%fused_computation.126 | convolution fusion | flops 167772160 | bytes 4521984 | tf_op jit(solution)/shard_map/dot_general | solution.py:92
  115.4 0.2 fusion.66
  115.6 15.5 %all-reduce.2 = (bf16[40,1024]{1,0:T(8,128)(2,1)S(1)}, bf16[40,64]{1,0:T(8,128)(2,1)S(1)}) all-reduce(f32[40,1024]{1,0:T(8,128)S(1)} %fusion.67, f32[40,64]{1,0:T(8,128)S(1)} %fusion.66), channel_id=1, replica_groups=mesh['groups'=2,'wide'=4,'narrow'=4] {'narrow'}, use_global_device_ids=true, to_apply=%region_2.0 | all-reduce | flops 43520 | bytes 261120 | tf_op jit(solution)/shard_map/psum | solution.py:100
  131.2 0.6 copy-done.9
  131.8 1.0 divide_multiply_fusion
  132.8 0.1 stack.24
  132.9 0.1 stack.25
  133.0 0.7 copy.203
  133.7 0.7 copy.205
  134.4 0.7 copy.207
  135.1 0.7 copy.209
  135.8 0.2 copy.242
  136.0 0.2 copy.243
  136.2 0.9 copy.244
  137.1 0.7 copy.202
  137.8 0.6 convert_element_type.253
  138.4 0.6 multiply_exponential_fusion
  139.1 0.1 fusion.64
  139.2 0.1 copy_bitcast_fusion
  139.3 0.2 broadcast_in_dim.8
  139.5 0.3 slice_bitcast_fusion.2
  139.8 0.2 broadcast_in_dim.7
  140.0 1.8 slice_bitcast_fusion.3
  141.8 7.8 %reduce-scatter.3.cloned.1.call-done = f32[16,2,40,64]{3,2,1,0:T(8,128)} async-done(((f32[64,2,40,64]{3,2,1,0:T(8,128)}), f32[16,2,40,64]{3,2,1,0:T(8,128)}) %reduce-scatter.3.cloned.1.call-update) | async-done | bytes 327696 | tf_op jit(solution)/shard_map/reduce_scatter | solution.py:94
  149.6 1.3 copy.268
  150.9 0.7 copy-done.4
  151.7 0.7 copy-done.5
  152.4 0.7 fusion.63
  153.0 1.8 copy.245
  154.8 1.8 copy.246
  156.6 2.0 multiply_multiply_fusion.1
  158.7 21.2 %multiply_reduce_fusion = (f32[20,64,16]{2,1,0:T(8,128)S(1)}, f32[20,64,16,256]{3,2,1,0:T(8,128)}, f32[20,64,16]{2,1,0:T(8,128)S(1)}) fusion(f32[20,64,256]{2,1,0:T(8,128)S(1)} %get-tuple-element.10, f32[20,64,256]{2,1,0:T(8,128)} %get-tuple-element.12, f32[20,64,16]{2,1,0:T(8,128)S(1)} %get-tuple-element.16, f32[20,64,256]{2,1,0:T(8,128)} %get-tuple-element.11, ...), kind=kLoop, calls=%fused_computation | loop fusion | flops 52387840 | bytes 47523840 | tf_op jit(solution)/shard_map/reduce_sum | solution.py:61
  180.0 0.8 bitcast_add_fusion.1
  180.7 0.4 stack.29
  181.1 0.2 copy.222
  181.3 0.4 stack.30
  181.7 0.2 copy.223
  181.9 0.1 pad_maximum_fusion.2
  182.0 0.5 stack.32
  182.5 0.4 copy.225
  182.9 1.1 fusion.47
  184.0 0.1 reduce_sum.43
  184.1 0.1 reduce_sum.44
  184.2 0.1 copy.228
  184.3 5.7 %psum.23 = f32[20,2,2]{0,2,1:T(2,128)S(1)} all-reduce(f32[20,2,2]{0,2,1:T(2,128)S(1)} %copy.228), channel_id=1, replica_groups=mesh['groups'=2,'wide'=4,'narrow'=4] {'narrow'}, use_global_device_ids=true, to_apply=%region_7.8 | all-reduce | flops 80 | bytes 640 | tf_op jit(solution)/shard_map/psum | solution.py:142
  190.0 0.1 copy.229
  190.2 0.1 mul.503
  190.3 0.1 mul.504
  190.4 1.1 fusion.46
  191.5 1.7 collective-permute-start
  193.2 2.2 collective-permute-start.1
  195.4 5.1 %collective-permute-done = bf16[40,64,16]{1,2,0:T(8,128)(2,1)S(1)} collective-permute-done((bf16[40,64,16]{1,2,0:T(8,128)(2,1)S(1)}, bf16[40,64,16]{1,2,0:T(8,128)(2,1)S(1)}, u32[]{:S(2)}, u32[]{:S(2)}) %collective-permute-start) | collective-permute-done | bytes 81952 | tf_op jit(solution)/shard_map/ppermute | solution.py:19
  200.5 1.8 dynamic_update_slice.12
  202.4 3.8 %dynamic_update_slice.13 = bf16[40,256,16]{1,0,2:T(8,128)(2,1)S(1)} dynamic-update-slice(bf16[40,256,16]{1,0,2:T(8,128)(2,1)S(1)} %dynamic_update_slice.12, bf16[40,64,16]{1,0,2:T(8,128)(2,1)S(1)} %copy.231, s32[]{:T(128)} %constant.49.clone.1, s32[]{:T(128)S(6)} %select_n.54, s32[]{:T(128)} %constant.49.clone.1) | dynamic-update-slice | bytes 163844 | tf_op jit(solution)/shard_map/dynamic_update_slice | solution.py:20
  206.3 4.0 %dynamic_update_slice.14 = bf16[40,256,16]{1,0,2:T(8,128)(2,1)S(1)} dynamic-update-slice(bf16[40,256,16]{1,0,2:T(8,128)(2,1)S(1)} %dynamic_update_slice.13, bf16[40,64,16]{1,0,2:T(8,128)(2,1)S(1)} %copy.232, s32[]{:T(128)} %constant.49.clone.1, s32[]{:T(128)S(6)} %select_n.56, s32[]{:T(128)} %constant.49.clone.1) | dynamic-update-slice | bytes 163844 | tf_op jit(solution)/shard_map/dynamic_update_slice | solution.py:23
  210.5 1.6 dynamic_update_slice.15
  212.1 28.5 %fusion.5 = bf16[40,2048]{1,0:T(8,128)(2,1)} fusion(bf16[40,256,16]{1,0,2:T(8,128)(2,1)S(1)} %dynamic_update_slice.15, bf16[256,16,2048]{2,1,0:T(8,128)(2,1)} %param.30), kind=kOutput, calls=%fused_computation.7 | convolution fusion | flops 671170560 | bytes 17268736 | tf_op jit(solution)/shard_map/rhc,hcd->rd/dot_general | solution.py:150
  240.7 0.7 pad_maximum_fusion.3
  241.4 0.7 pad_maximum_fusion.1
  242.1 19.4 %reduce-scatter.5.cloned.1.call-done = bf16[40,512]{1,0:T(8,128)(2,1)} async-done(((bf16[40,2048]{1,0:T(8,128)(2,1)}), bf16[40,512]{1,0:T(8,128)(2,1)}) %reduce-scatter.5.cloned.1.call-update) | async-done | bytes 40976 | tf_op jit(solution)/shard_map/reduce_scatter | solution.py:156
  261.5 1.4 reshape.330
  (77 shorter events, 0.8 us)
Async XLA Ops:
  7.2 108.2 %copy-start = (bf16[2048,64]{0,1:T(8,128)(2,1)S(1)}, bf16[2048,64]{0,1:T(8,128)(2,1)}, u32[]{:S(2)}) copy-start(bf16[2048,64]{0,1:T(8,128)(2,1)} %param.19) | copy-start | bytes 786436
  7.2 81.0 %copy-start.11 = (bf16[20,2,2048]{2,1,0:T(2,128)(2,1)S(1)}, bf16[20,2,2048]{2,1,0:T(2,128)(2,1)}, u32[]{:S(2)}) copy-start(bf16[20,2,2048]{2,1,0:T(2,128)(2,1)} %param.16) | copy-start | bytes 491524
  7.2 142.4 %reduce-scatter.3.cloned.1.call-start = ((), (), s32[]{:S(2)}) async-start(), calls=%async_computation.2 | async-start | bytes 3276800 | tf_op jit(solution)/shard_map/reduce_scatter | solution.py:94
  88.3 42.9 %copy-start.22 = (bf16[1024]{0:T(1024)(128)(2,1)S(1)}, bf16[1024]{0:T(1024)(128)(2,1)}, u32[]{:S(2)}) copy-start(bf16[1024]{0:T(1024)(128)(2,1)} %param.23) | copy-start | bytes 6148
  88.3 42.9 %copy-start.18 = (bf16[4,1024]{1,0:T(4,128)(2,1)S(1)}, bf16[4,1024]{1,0:T(4,128)(2,1)}, u32[]{:S(2)}) copy-start(bf16[4,1024]{1,0:T(4,128)(2,1)} %param.22) | copy-start | bytes 24580
  88.3 44.7 %copy-start.25 = (f32[64]{0:T(128)S(1)}, f32[64]{0:T(128)}, u32[]{:S(2)}) copy-start(f32[64]{0:T(128)} %param.27) | copy-start | bytes 772
  88.3 44.7 %copy-start.19 = (bf16[4,64,16]{1,2,0:T(8,128)(2,1)S(1)}, bf16[4,64,16]{1,2,0:T(8,128)(2,1)}, u32[]{:S(2)}) copy-start(bf16[4,64,16]{1,2,0:T(8,128)(2,1)} %param.20) | copy-start | bytes 24580
  88.3 47.4 %copy-start.7 = (bf16[20,3,64,16]{2,3,1,0:T(8,128)(2,1)S(1)}, bf16[20,3,64,16]{2,3,1,0:T(8,128)(2,1)}, u32[]{:S(2)}) copy-start(bf16[20,3,64,16]{2,3,1,0:T(8,128)(2,1)} %param.24) | copy-start | bytes 368644
  88.3 48.8 %copy-start.20 = (bf16[64,16]{0,1:T(8,128)(2,1)S(1)}, bf16[64,16]{0,1:T(8,128)(2,1)}, u32[]{:S(2)}) copy-start(bf16[64,16]{0,1:T(8,128)(2,1)} %param.21) | copy-start | bytes 6148
  88.3 49.4 %copy-start.21 = (bf16[64,16]{0,1:T(8,128)(2,1)S(1)}, bf16[64,16]{0,1:T(8,128)(2,1)}, u32[]{:S(2)}) copy-start(bf16[64,16]{0,1:T(8,128)(2,1)} %param.29) | copy-start | bytes 6148
  110.1 28.4 %copy-start.23 = (f32[64]{0:T(128)S(1)}, f32[64]{0:T(128)}, u32[]{:S(2)}) copy-start(f32[64]{0:T(128)} %param.26) | copy-start | bytes 772
  112.2 149.3 %reduce-scatter.5.cloned.1.call-start = ((), (), s32[]{:S(2)}) async-start(), calls=%async_computation.3 | async-start | bytes 204800 | tf_op jit(solution)/shard_map/reduce_scatter | solution.py:156
  131.1 0.6 copy-start.9
  150.9 0.7 copy-start.4
  151.7 0.7 copy-start.5
  158.6 21.3 %copy-start.1 = (bf16[20,1,64,16]{3,2,0,1:T(8,128)(2,1)S(1)}, bf16[20,1,64,16]{3,2,0,1:T(8,128)(2,1)}, u32[]{:S(2)}) copy-start(bf16[20,1,64,16]{3,2,0,1:T(8,128)(2,1)} %copy.244) | copy-start | bytes 122884
  158.6 21.3 %copy-start.2 = (bf16[20,1,64,16]{3,2,0,1:T(8,128)(2,1)S(1)}, bf16[20,1,64,16]{3,2,0,1:T(8,128)(2,1)}, u32[]{:S(2)}) copy-start(bf16[20,1,64,16]{3,2,0,1:T(8,128)(2,1)} %copy.245) | copy-start | bytes 122884
  158.6 21.3 %copy-start.3 = (bf16[20,1,64,16]{3,2,0,1:T(8,128)(2,1)S(1)}, bf16[20,1,64,16]{3,2,0,1:T(8,128)(2,1)}, u32[]{:S(2)}) copy-start(bf16[20,1,64,16]{3,2,0,1:T(8,128)(2,1)} %copy.246) | copy-start | bytes 122884
  158.6 21.3 %copy-start.13 = (f32[64,16]{1,0:T(8,128)S(1)}, f32[64,16]{1,0:T(8,128)}, u32[]{:S(2)}) copy-start(f32[64,16]{1,0:T(8,128)} %copy.203) | copy-start | bytes 12292
  158.6 21.3 %copy-start.14 = (f32[64,16]{1,0:T(8,128)S(1)}, f32[64,16]{1,0:T(8,128)}, u32[]{:S(2)}) copy-start(f32[64,16]{1,0:T(8,128)} %copy.205) | copy-start | bytes 12292
  158.6 21.3 %copy-start.15 = (f32[64,16]{1,0:T(8,128)S(1)}, f32[64,16]{1,0:T(8,128)}, u32[]{:S(2)}) copy-start(f32[64,16]{1,0:T(8,128)} %copy.207) | copy-start | bytes 12292
  158.6 21.3 %copy-start.16 = (f32[64,16]{1,0:T(8,128)S(1)}, f32[64,16]{1,0:T(8,128)}, u32[]{:S(2)}) copy-start(f32[64,16]{1,0:T(8,128)} %copy.209) | copy-start | bytes 12292
  158.6 21.3 %copy-start.17 = (f32[64,16]{1,0:T(8,128)S(1)}, f32[64,16]{1,0:T(8,128)}, u32[]{:S(2)}) copy-start(f32[64,16]{1,0:T(8,128)} %copy.202) | copy-start | bytes 12292
  158.6 21.3 %copy-start.24 = (f32[64]{0:T(128)S(1)}, f32[64]{0:T(128)}, u32[]{:S(2)}) copy-start(f32[64]{0:T(128)} %param.28) | copy-start | bytes 772
  179.9 60.8 %copy-start.10 = (bf16[20,2,1024]{2,0,1:T(8,128)(2,1)S(1)}, bf16[20,2,1024]{2,0,1:T(8,128)(2,1)}, u32[]{:S(2)}) copy-start(bf16[20,2,1024]{2,0,1:T(8,128)(2,1)} %copy-done.9) | copy-start | bytes 245764
  179.9 60.8 %copy-start.12 = (bf16[20,3,1024]{2,0,1:T(8,128)(2,1)S(1)}, bf16[20,3,1024]{2,0,1:T(8,128)(2,1)}, u32[]{:S(2)}) copy-start(bf16[20,3,1024]{2,0,1:T(8,128)(2,1)} %param.25) | copy-start | bytes 368644
  179.9 61.4 %copy-start.6 = (bf16[1,40,64,16]{2,3,1,0:T(8,128)(2,1)S(1)}, bf16[1,40,64,16]{2,3,1,0:T(8,128)(2,1)}, u32[]{:S(2)}) copy-start(bf16[1,40,64,16]{2,3,1,0:T(8,128)(2,1)} %copy-done.5) | copy-start | bytes 245764
  179.9 61.4 %copy-start.8 = (bf16[20,3,64,16]{2,3,1,0:T(8,128)(2,1)S(1)}, bf16[20,3,64,16]{2,3,1,0:T(8,128)(2,1)}, u32[]{:S(2)}) copy-start(bf16[20,3,64,16]{2,3,1,0:T(8,128)(2,1)} %param.24) | copy-start | bytes 368644
  191.5 9.0 %collective-permute-start = (bf16[40,64,16]{1,2,0:T(8,128)(2,1)S(1)}, bf16[40,64,16]{1,2,0:T(8,128)(2,1)S(1)}, u32[]{:S(2)}, u32[]{:S(2)}) collective-permute-start(bf16[40,64,16]{1,2,0:T(8,128)(2,1)S(1)} %fusion.46), channel_id=1, source_target_pairs={{0,4},{4,8},{8,12},{12,0},{1,5},{5,9},{9,13},{13,1},{2,6},{6,10},{... | collective-permute-start | bytes 245768 | tf_op jit(solution)/shard_map/ppermute | solution.py:19
  193.2 13.1 %collective-permute-start.1 = (bf16[40,64,16]{1,2,0:T(8,128)(2,1)S(1)}, bf16[40,64,16]{1,2,0:T(8,128)(2,1)S(1)}, u32[]{:S(2)}, u32[]{:S(2)}) collective-permute-start(bf16[40,64,16]{1,2,0:T(8,128)(2,1)S(1)} %fusion.46), channel_id=1, source_target_pairs={{0,12},{4,0},{8,4},{12,8},{1,13},{5,1},{9,5},{13,9},{2,14},{6,2},{... | collective-permute-start | bytes 245768 | tf_op jit(solution)/shard_map/ppermute | solution.py:22
  200.4 9.9 %collective-permute-start.2 = (bf16[40,64,16]{1,2,0:T(8,128)(2,1)S(1)}, bf16[40,64,16]{1,2,0:T(8,128)(2,1)S(1)}, u32[]{:S(2)}, u32[]{:S(2)}) collective-permute-start(bf16[40,64,16]{1,2,0:T(8,128)(2,1)S(1)} %collective-permute-done), channel_id=1, source_target_pairs={{0,4},{4,8},{8,12},{12,0},{1,5},{5,9},{9,13},{13,1},{2,6},{6,10},{... | collective-permute-start | bytes 245768 | tf_op jit(solution)/shard_map/ppermute | solution.py:19
Sparse Core Ops, SparseCore 0:
  112.3 37.2 reduce-scatter.2
  240.8 20.6 reduce-scatter.4
